TPU v7x, 256 devices: a whole 4x4x8 slice. The times are simulated.
256 devices in a mesh: space: 64 (over x, z, core), slab: 4 (over y).
Axes of the slice: x: 4, y: 4, z: 8, core: 2. Of those that a mesh axis runs over, the one named last changes fastest.
Arguments:
- tokens: float32 [65536, 512], P(('space', 'slab')), may hold values from -6 to 6
- gain: float32 [512], replicated, may hold values from 0.25 to 1.75
- query_weight: float32 [512, 512], replicated, may hold values from -3.1 to 3.1
- key_weight: float32 [512, 512], replicated, may hold values from -0.25 to 0.25
- value_weight: float32 [512, 512], replicated, may hold values from -0.25 to 0.25
- output_weight: float32 [512, 512], replicated, may hold values from -0.25 to 0.25
- neighbour_list: int32 [512, 3], P(('space', 'slab')), may hold values from 0 to 5, as said below
- neighbour_count: int32 [512], P(('space', 'slab')), may hold values from 1 to 3, as said below
- cotangent: float32 [65536, 512], P(('space', 'slab')), may hold values from -6 to 6
Outputs:
- result: float32 [65536, 512], P(('space', 'slab'))
- d_tokens: float32 [65536, 512], P(('space', 'slab'))
- d_gain: float32 [512], replicated
- d_query: float32 [512, 512], replicated
- d_key: float32 [512, 512], replicated
- d_value: float32 [512, 512], replicated
- d_output: float32 [512, 512], replicated
Inputs may be any that keep to these rules, and one draw needn't show every extreme that they name: `neighbour_list`: each row holds distinct window indices, never the patch's own index 2 + p % 2. Only the first neighbour_count[p] entries of a row are live.
All inputs are finite; a program needn't handle non-finite values.
Results may differ from a plain program's by a relative error of at most 0.0003.
Values sent between devices are 32-bit elements; how exact they have to be, the bound alone decides.
A program may use at most 128 MiB of HBM per device.

v0:
```python
import jax
import jax.numpy as jnp
from jax import lax
from jax.sharding import PartitionSpec as P

HEADS = 8
PT = 128


def extended(cells, sides, width):
    for axis, dim in sides:
        count = lax.axis_size(axis)
        head = lax.slice_in_dim(cells, 0, width, axis=dim)
        tail = lax.slice_in_dim(cells, cells.shape[dim] - width, cells.shape[dim], axis=dim)
        cells = jnp.concatenate(
            [
                lax.ppermute(tail, axis, [(i, (i + 1) % count) for i in range(count)]),
                cells,
                lax.ppermute(head, axis, [((i + 1) % count, i) for i in range(count)]),
            ],
            axis=dim,
        )
    return cells


def passed_along(value, axis, steps):
    count = lax.axis_size(axis)
    pairs = [(source, (source + steps) % count) for source in range(count)]
    return lax.ppermute(value, axis, pairs)


def matmul(left, right):
    return jnp.dot(left, right, precision=lax.Precision.HIGHEST, preferred_element_type=jnp.float32)


def normalize(tokens, gain):
    row_mean = jnp.mean(tokens, axis=1, keepdims=True)
    centred = tokens - row_mean
    variance = jnp.mean(centred * centred, axis=1, keepdims=True)
    return centred * lax.rsqrt(variance + 1e-05) * gain[None, :]


def attention(query, key_win, value_win, block_index, live_mask):
    patch_count = block_index.shape[0]
    model_width = query.shape[1]
    head_dim = model_width // HEADS
    picked_keys = key_win.reshape(-1, PT, model_width)[block_index].reshape(
        patch_count, -1, HEADS, head_dim
    )
    picked_values = value_win.reshape(-1, PT, model_width)[block_index].reshape(
        patch_count, -1, HEADS, head_dim
    )
    query_blocks = query.reshape(patch_count, PT, HEADS, head_dim)
    scores = jnp.einsum(
        "pqhd,pkhd->phqk", query_blocks, picked_keys, precision=lax.Precision.HIGHEST
    ) * head_dim ** (-0.5)
    key_mask = jnp.repeat(live_mask, PT, axis=1)
    scores = jnp.where(key_mask[:, None, None, :], scores, -1e30)
    row_max = jnp.max(scores, axis=3, keepdims=True)
    weights = jnp.exp(scores - row_max)
    probability = weights / jnp.sum(weights, axis=3, keepdims=True)
    mixed = jnp.einsum(
        "phqk,pkhd->pqhd", probability, picked_values, precision=lax.Precision.HIGHEST
    )
    return mixed.reshape(patch_count * PT, model_width)


def body(
    tokens,
    gain,
    query_weight,
    key_weight,
    value_weight,
    output_weight,
    neighbour_list,
    neighbour_count,
    cotangent,
):
    row_count = tokens.shape[0]
    model_width = tokens.shape[1]
    patch_count = neighbour_list.shape[0]
    hidden, norm_pull = jax.vjp(normalize, tokens, gain)
    query = matmul(hidden, query_weight)
    own_blocks = patch_count + jnp.arange(patch_count, dtype=jnp.int32)
    block_index = jnp.concatenate([own_blocks[:, None], neighbour_list], axis=1)
    slot_ids = jnp.arange(neighbour_list.shape[1], dtype=jnp.int32)
    live_mask = jnp.concatenate(
        [jnp.ones((patch_count, 1), dtype=bool), slot_ids[None, :] < neighbour_count[:, None]],
        axis=1,
    )
    key_rows = matmul(hidden, key_weight)
    value_rows = matmul(hidden, value_weight)
    window = extended(jnp.concatenate([key_rows, value_rows], axis=1), (("space", 0),), row_count)
    key_win = window[:, :model_width]
    value_win = window[:, model_width:]

    def local_attention(query_rows, key_part, value_part):
        return attention(query_rows, key_part, value_part, block_index, live_mask)

    mixed, attention_pull = jax.vjp(local_attention, query, key_win, value_win)
    result = matmul(mixed, output_weight) + tokens
    grad_output = matmul(mixed.T, cotangent)
    d_mixed = matmul(cotangent, output_weight.T)
    d_queries, d_key_win, d_value_win = attention_pull(d_mixed)
    grad_query = matmul(hidden.T, d_queries)
    d_window = jnp.concatenate([d_key_win, d_value_win], axis=1)
    d_owned = d_window[row_count : 2 * row_count]
    for offset, halo_part in ((-1, d_window[:row_count]), (1, d_window[2 * row_count :])):
        d_owned = d_owned + passed_along(halo_part, "space", offset)
    d_keys = d_owned[:, :model_width]
    d_values = d_owned[:, model_width:]
    grad_key = matmul(hidden.T, d_keys)
    grad_value = matmul(hidden.T, d_values)
    d_hidden = (
        matmul(d_queries, query_weight.T)
        + matmul(d_keys, key_weight.T)
        + matmul(d_values, value_weight.T)
    )
    d_norm, grad_gain = norm_pull(d_hidden)
    d_tokens = d_norm + cotangent
    grad_gain, grad_query, grad_key, grad_value, grad_output = lax.psum(
        (grad_gain, grad_query, grad_key, grad_value, grad_output), ("space", "slab")
    )
    return (result, d_tokens, grad_gain, grad_query, grad_key, grad_value, grad_output)


def solution(mesh):
    return jax.shard_map(
        body,
        mesh=mesh,
        in_specs=(
            P(("space", "slab"), None),
            P(),
            P(),
            P(),
            P(),
            P(),
            P(("space", "slab"), None),
            P(("space", "slab")),
            P(("space", "slab"), None),
        ),
        out_specs=(P(("space", "slab"), None), P(("space", "slab"), None), P(), P(), P(), P(), P()),
        check_vma=False,
    )
```

profile of v0, /device:TPU:8, one launch (start us, length us, event | category | flops | bytes accessed | tf_op | source)
XLA Modules:
  0.0 428.7 jit_solution(7895990466346102938)
XLA Ops:
  9.8 2.2 fusion.56
  12.0 2.6 fusion.57
  15.6 7.5 %collective-permute-start.1 = (f32[256,1024]{1,0:T(8,128)}, f32[256,1024]{1,0:T(8,128)}, u32[]{:S(2)}, u32[]{:S(2)}) collective-permute-start(f32[256,1024]{1,0:T(8,128)} %pad_maximum_fusion.2), channel_id=1, source_target_pairs={{4,0},{8,4},{12,8},{16,12},{20,16},{24,20},{28,24},{32,28},{36,32}... | collective-permute-start | bytes 3145736 | tf_op jit(solution)/shard_map/ppermute | solution.py:19
  23.6 3.9 fusion.55
  29.7 3.0 fusion.62
  35.7 5.2 %collective-permute-done = f32[256,1024]{1,0:T(8,128)} collective-permute-done((f32[256,1024]{1,0:T(8,128)}, f32[256,1024]{1,0:T(8,128)}, u32[]{:S(2)}, u32[]{:S(2)}) %collective-permute-start) | collective-permute-done | bytes 1048608 | tf_op jit(solution)/shard_map/ppermute | solution.py:17
  44.3 3.4 gather_fusion
  47.8 4.9 %reshape.226 = f32[2,512,8,64]{3,2,1,0:T(8,128)} reshape(f32[8,128,512]{2,1,0:T(8,128)} %gather_fusion) | data formatting | bytes 4194304 | tf_op jit(solution)/shard_map/jvp()/reshape | solution.py:50
  52.6 3.8 copy.41
  58.4 4.4 %reshape.227 = f32[2,512,8,64]{3,2,1,0:T(8,128)} reshape(f32[8,128,512]{2,1,0:T(8,128)} %gather_fusion.1) | data formatting | bytes 4194304 | tf_op jit(solution)/shard_map/jvp()/reshape | solution.py:47
  62.8 3.9 copy.40
  66.7 5.7 %fusion.1 = (f32[2,8,128]{2,1,0:T(8,128)S(1)}, f32[2,8,128,512]{3,2,1,0:T(8,128)S(1)}) fusion(pred[2,512]{1,0:T(4,128)(4,1)S(1)} %bitcast.73, f32[2,512,8,64]{1,3,2,0:T(8,128)} %copy.40, f32[2,128,8,64]{1,0,3,2:T(2,128)S(1)} %copy-done.9), kind=kOutput, calls=%fused_computation.15 | convolution fusion | flops 808450048 | bytes 6824960 | tf_op jit(solution)/shard_map/jvp(pqhd,pkhd->phqk)/dot_general | solution.py:54
  73.8 4.4 %fusion.14 = f32[2,512,8,64]{1,3,2,0:T(8,128)} fusion(f32[2,8,128]{2,1,0:T(8,128)S(1)} %fusion.45, f32[2,8,64,128]{3,0,2,1:T(2,128)S(1)} %bitcast.71, f32[2,8,128,512]{3,2,1,0:T(8,128)S(1)} %get-tuple-element.25, f32[2,8,128]{2,1,0:T(8,128)S(1)} %get-tuple-element.24, pred[2,512]{1,0:T(4,128)(4,1)S(1)} %bitcast.75), kind=kOutput, calls=%fused_computation.30 | convolution fusion | flops 809500672 | bytes 6833152 | tf_op jit(solution)/shard_map/transpose(jvp(phqk,pkhd->pqhd))/dot_general | solution.py:62
  78.2 5.6 %convert_reduce_fusion = (f32[2,8,128]{2,1,0:T(8,128)S(1)}, pred[2,8,128,512]{3,2,1,0:T(32,128)(4,1)S(1)}, f32[2,8,128]{2,1,0:T(8,128)S(1)}, f32[2,8,128,512]{3,2,1,0:T(8,128)S(1)}) fusion(f32[2,8,128]{2,1,0:T(8,128)S(1)} %get-tuple-element.24, f32[2,8,128,512]{3,2,1,0:T(8,128)S(1)} %get-tuple-element.25, pred[2,512]{1,0:T(4,128)(4,1)S(1)} %bitcast.76, ...), kind=kOutput, calls=%fused_computation.5 | convolution fusion | flops 814739456 | bytes 12092416 | tf_op jit(solution)/shard_map/transpose(jvp(phqk,pkhd->pqhd))/dot_general | solution.py:62
  83.9 2.2 fusion.59
  88.0 4.6 %fusion.15 = f32[2,512,8,64]{1,3,2,0:T(8,128)} fusion(f32[2,8,128,512]{3,2,1,0:T(8,128)S(1)} %get-tuple-element.16, pred[2,8,128,512]{3,2,1,0:T(32,128)(4,1)S(1)} %get-tuple-element.18, f32[2,8,128]{2,1,0:T(8,128)S(1)} %negate_divide_fusion, pred[2,512]{1,0:T(4,128)(4,1)S(1)} %bitcast.78, f32[2,128,8,64]{1,0,3,2:T(2,128)S(1)} %copy-done.9), kind=kOutput, calls=%fused_computation.31 | convolution fusion | flops 809500672 | bytes 7873536 | tf_op jit(solution)/shard_map/transpose(jvp(pqhd,pkhd->phqk))/dot_general | solution.py:54
  92.6 3.8 copy.56
  96.5 4.8 %reshape.224 = f32[8,128,512]{2,1,0:T(8,128)} reshape(f32[2,512,8,64]{3,2,1,0:T(8,128)} %copy.56) | data formatting | bytes 4194304 | tf_op jit(solution)/shard_map/transpose(jvp())/reshape | solution.py:47
  101.3 3.8 copy.57
  105.1 4.8 %reshape.225 = f32[8,128,512]{2,1,0:T(8,128)} reshape(f32[2,512,8,64]{3,2,1,0:T(8,128)} %copy.57) | data formatting | bytes 4194304 | tf_op jit(solution)/shard_map/transpose(jvp())/reshape | solution.py:50
  111.3 5.0 %scatter_fusion = f32[6,128,512]{2,1,0:T(8,128)} fusion(f32[6,128,512]{2,1,0:T(8,128)} %broadcast.104.clone, s32[8]{0:T(128)S(1)} %reshape.186, f32[8,128,512]{2,1,0:T(8,128)} %reshape.224), kind=kCustom, calls=%fused_computation.2 | custom fusion | flops 524288 | bytes 6291488 | tf_op jit(solution)/shard_map/transpose(jvp())/scatter-add | solution.py:47
  116.5 3.4 scatter_fusion.1
  121.6 5.0 %collective-permute-start.2 = (f32[256,1024]{1,0:T(8,128)S(1)}, f32[256,1024]{1,0:T(8,128)S(1)}, u32[]{:S(2)}, u32[]{:S(2)}) collective-permute-start(f32[256,1024]{1,0:T(8,128)S(1)} %get-tuple-element.20), channel_id=1, source_target_pairs={{0,252},{4,0},{8,4},{12,8},{16,12},{20,16},{24,20},{28,24},{32,28}... | collective-permute-start | bytes 3145736 | tf_op jit(solution)/shard_map/ppermute | solution.py:29
  126.6 6.9 %fusion.16 = f32[2,128,8,64]{1,3,2,0:T(8,128)S(1)} fusion(f32[2,512,8,64]{1,3,2,0:T(8,128)} %copy.41, f32[2,8,128]{2,1,0:T(8,128)S(1)} %fusion.45, f32[2,8,128,512]{3,2,1,0:T(8,128)S(1)} %copy-done.5, f32[2,8,128]{2,1,0:T(8,128)S(1)} %get-tuple-element.24, pred[2,512]{1,0:T(4,128)(4,1)S(1)} %bitcast.79), kind=kOutput, calls=%fused_computation.32 | convolution fusion | flops 809500672 | bytes 6833152 | tf_op jit(solution)/shard_map/jvp(phqk,pkhd->pqhd)/dot_general | solution.py:62
  134.0 5.6 %fusion.17 = f32[2,128,8,64]{1,3,2,0:T(8,128)S(1)} fusion(f32[2,512,8,64]{1,3,2,0:T(8,128)S(1)} %copy-done.6, f32[2,8,128,512]{3,2,1,0:T(8,128)S(1)} %copy-done.3, pred[2,8,128,512]{3,2,1,0:T(32,128)(4,1)S(1)} %copy-done.17, f32[2,8,128]{2,1,0:T(8,128)S(1)} %negate_divide_fusion, pred[2,512]{1,0:T(4,128)(4,1)S(1)} %bitcast.80), kind=kOutput, calls=%fused_computation.36 | convolution fusion | flops 809500672 | bytes 7873536 | tf_op jit(solution)/shard_map/transpose(jvp(pqhd,pkhd->phqk))/dot_general | solution.py:54
  142.0 2.9 fusion.22
  150.6 3.6 fusion.24
  154.2 3.1 convolution_add_fusion.2
  160.3 72.0 %psum.35 = f32[512]{0:T(512)} all-reduce(f32[512]{0:T(512)S(1)} %get-tuple-element.7), channel_id=1, replica_groups=mesh['space'=64,'slab'=4] {'space','slab'}, use_global_device_ids=true, to_apply=%region_12.13 | all-reduce | flops 512 | bytes 4096 | tf_op jit(solution)/shard_map/psum | solution.py:121
  234.5 180.3 %all-reduce.4.cloned.1.call-done = (f32[512,512]{1,0:T(8,128)}, f32[512,512]{1,0:T(8,128)}, f32[512,512]{1,0:T(8,128)}, f32[512,512]{1,0:T(8,128)}) async-done(((f32[512,512]{1,0:T(8,128)}, f32[512,512]{1,0:T(8,128)}, f32[512,512]{1,0:T(8,128)}, f32[512,512]{1,0:T(8,128)}), (f32[512,512]{1,0:T(8,128)}, f32[512,512]{1,0:T(8,128)}, f32[512,512]{1,0:T(8,128)}, ...) | async-done | bytes 4194320 | tf_op jit(solution)/shard_map/psum | solution.py:121
  414.8 2.4 copy.107
  417.2 2.3 copy.108
  (99 shorter events, 36.8 us)
Async XLA Ops:
  7.2 2.6 copy-start
  7.2 16.4 %copy-start.1 = (f32[256,512]{1,0:T(8,128)S(1)}, f32[256,512]{1,0:T(8,128)}, u32[]{:S(2)}) copy-start(f32[256,512]{1,0:T(8,128)} %param.9) | copy-start | bytes 1572868
  7.2 16.4 %copy-start.23 = (f32[512]{0:T(512)S(1)}, f32[512]{0:T(512)}, u32[]{:S(2)}) copy-start(f32[512]{0:T(512)} %param.10) | copy-start | bytes 6148
  7.2 16.0 %copy-start.24 = (s32[2,3]{1,0:T(2,128)S(1)}, s32[2,3]{1,0:T(2,128)}, u32[]{:S(2)}) copy-start(s32[2,3]{1,0:T(2,128)} %param.15) | copy-start | bytes 76
  7.2 16.2 %copy-start.25 = (s32[2]{0:T(128)S(1)}, s32[2]{0:T(128)}, u32[]{:S(2)}) copy-start(s32[2]{0:T(128)} %param.16) | copy-start | bytes 28
  7.2 407.6 %all-reduce.4.cloned.1.call-start = ((), (), s32[]{:S(2)}) async-start(), calls=%async_computation | async-start | bytes 8388608 | tf_op jit(solution)/shard_map/psum | solution.py:121
  12.0 17.7 %copy-start.13 = (f32[256,512]{1,0:T(8,128)S(1)}, f32[256,512]{1,0:T(8,128)}, u32[]{:S(2)}) copy-start(f32[256,512]{1,0:T(8,128)} %param.17) | copy-start | bytes 1572868
  15.6 20.1 %collective-permute-start.1 = (f32[256,1024]{1,0:T(8,128)}, f32[256,1024]{1,0:T(8,128)}, u32[]{:S(2)}, u32[]{:S(2)}) collective-permute-start(f32[256,1024]{1,0:T(8,128)} %pad_maximum_fusion.2), channel_id=1, source_target_pairs={{4,0},{8,4},{12,8},{16,12},{20,16},{24,20},{28,24},{32,28},{36,32}... | collective-permute-start | bytes 3145736 | tf_op jit(solution)/shard_map/ppermute | solution.py:19
  23.1 17.9 %collective-permute-start = (f32[256,1024]{1,0:T(8,128)}, f32[256,1024]{1,0:T(8,128)}, u32[]{:S(2)}, u32[]{:S(2)}) collective-permute-start(f32[256,1024]{1,0:T(8,128)} %pad_maximum_fusion.2), channel_id=1, source_target_pairs={{0,4},{4,8},{8,12},{12,16},{16,20},{20,24},{24,28},{28,32},{32,36}... | collective-permute-start | bytes 3145736 | tf_op jit(solution)/shard_map/ppermute | solution.py:17
  62.8 3.9 copy-start.9
  66.7 7.1 %copy-start.22 = (f32[2,128,8,64]{1,0,3,2:T(2,128)S(1)}, f32[2,128,8,64]{1,0,3,2:T(2,128)}, u32[]{:S(2)}) copy-start(f32[2,128,8,64]{1,0,3,2:T(2,128)} %reshape.178) | copy-start | bytes 1572868
  72.4 11.4 %copy-start.4 = (f32[2,8,128,512]{3,2,1,0:T(8,128)}, f32[2,8,128,512]{3,2,1,0:T(8,128)S(1)}, u32[]{:S(2)}) copy-start(f32[2,8,128,512]{3,2,1,0:T(8,128)S(1)} %get-tuple-element.25) | copy-start | bytes 12582916
  73.8 4.5 %copy-start.19 = (f32[2,512,8,64]{1,3,2,0:T(8,128)S(1)}, f32[2,512,8,64]{1,3,2,0:T(8,128)}, u32[]{:S(2)}) copy-start(f32[2,512,8,64]{1,3,2,0:T(8,128)} %copy.41) | copy-start | bytes 6291460
  83.8 2.2 copy-start.16
  86.0 2.0 copy-start.2
  119.9 6.7 %copy-start.5 = (f32[2,8,128,512]{3,2,1,0:T(8,128)S(1)}, f32[2,8,128,512]{3,2,1,0:T(8,128)}, u32[]{:S(2)}) copy-start(f32[2,8,128,512]{3,2,1,0:T(8,128)} %copy-done.4) | copy-start | bytes 12582916
  121.4 23.5 %collective-permute-start.3 = (f32[256,1024]{1,0:T(8,128)S(1)}, f32[256,1024]{1,0:T(8,128)S(1)}, u32[]{:S(2)}, u32[]{:S(2)}) collective-permute-start(f32[256,1024]{1,0:T(8,128)S(1)} %get-tuple-element.21), channel_id=1, source_target_pairs={{0,4},{4,8},{8,12},{12,16},{16,20},{20,24},{24,28},{28,32},{32,36}... | collective-permute-start | bytes 3145736 | tf_op jit(solution)/shard_map/ppermute | solution.py:29
  121.5 12.4 %copy-start.3 = (f32[2,8,128,512]{3,2,1,0:T(8,128)S(1)}, f32[2,8,128,512]{3,2,1,0:T(8,128)}, u32[]{:S(2)}) copy-start(f32[2,8,128,512]{3,2,1,0:T(8,128)} %copy-done.2) | copy-start | bytes 12582916
  121.5 12.4 %copy-start.6 = (f32[2,512,8,64]{1,3,2,0:T(8,128)S(1)}, f32[2,512,8,64]{1,3,2,0:T(8,128)}, u32[]{:S(2)}) copy-start(f32[2,512,8,64]{1,3,2,0:T(8,128)} %copy.40) | copy-start | bytes 6291460
  121.6 12.4 %copy-start.17 = (pred[2,8,128,512]{3,2,1,0:T(32,128)(4,1)S(1)}, pred[2,8,128,512]{3,2,1,0:T(32,128)(4,1)}, u32[]{:S(2)}) copy-start(pred[2,8,128,512]{3,2,1,0:T(32,128)(4,1)} %copy-done.16) | copy-start | bytes 3145732
  121.6 23.4 %collective-permute-start.2 = (f32[256,1024]{1,0:T(8,128)S(1)}, f32[256,1024]{1,0:T(8,128)S(1)}, u32[]{:S(2)}, u32[]{:S(2)}) collective-permute-start(f32[256,1024]{1,0:T(8,128)S(1)} %get-tuple-element.20), channel_id=1, source_target_pairs={{0,252},{4,0},{8,4},{12,8},{16,12},{20,16},{24,20},{28,24},{32,28}... | collective-permute-start | bytes 3145736 | tf_op jit(solution)/shard_map/ppermute | solution.py:29
  134.0 6.0 %copy-start.10 = (f32[2,128,8,64]{1,0,3,2:T(2,128)}, f32[2,128,8,64]{1,0,3,2:T(2,128)S(1)}, u32[]{:S(2)}) copy-start(f32[2,128,8,64]{1,0,3,2:T(2,128)S(1)} %copy.42) | copy-start | bytes 1572868
  134.0 6.0 %copy-start.14 = (f32[256,512]{1,0:T(8,128)S(1)}, f32[256,512]{1,0:T(8,128)}, u32[]{:S(2)}) copy-start(f32[256,512]{1,0:T(8,128)} %param.17) | copy-start | bytes 1572868
  140.0 5.0 %copy-start.12 = (f32[2,128,8,64]{1,0,3,2:T(2,128)}, f32[2,128,8,64]{1,0,3,2:T(2,128)S(1)}, u32[]{:S(2)}) copy-start(f32[2,128,8,64]{1,0,3,2:T(2,128)S(1)} %copy.47) | copy-start | bytes 1572868
  146.3 2.1 copy-start.7
  148.4 5.8 %copy-start.11 = (f32[2,128,8,64]{1,0,3,2:T(2,128)S(1)}, f32[2,128,8,64]{1,0,3,2:T(2,128)}, u32[]{:S(2)}) copy-start(f32[2,128,8,64]{1,0,3,2:T(2,128)} %copy-done.10) | copy-start | bytes 1572868
  150.5 6.8 %copy-start.8 = (f32[256,1024]{1,0:T(8,128)S(1)}, f32[256,1024]{1,0:T(8,128)}, u32[]{:S(2)}) copy-start(f32[256,1024]{1,0:T(8,128)} %copy-done.7) | copy-start | bytes 3145732
  150.6 6.8 %copy-start.18 = (f32[512,512]{1,0:T(8,128)S(1)}, f32[512,512]{1,0:T(8,128)}, u32[]{:S(2)}) copy-start(f32[512,512]{1,0:T(8,128)} %param.12) | copy-start | bytes 3145732
  157.3 76.3 %copy-start.15 = (f32[256,512]{1,0:T(8,128)S(1)}, f32[256,512]{1,0:T(8,128)}, u32[]{:S(2)}) copy-start(f32[256,512]{1,0:T(8,128)} %param.17) | copy-start | bytes 1572868
  414.8 4.7 %copy-start.21 = (f32[512,512]{1,0:T(8,128)S(1)}, f32[512,512]{1,0:T(8,128)}, u32[]{:S(2)}) copy-start(f32[512,512]{1,0:T(8,128)} %get-tuple-element.33) | copy-start | bytes 3145732
  414.8 5.7 %copy-start.20 = (f32[512,512]{1,0:T(8,128)S(1)}, f32[512,512]{1,0:T(8,128)}, u32[]{:S(2)}) copy-start(f32[512,512]{1,0:T(8,128)} %get-tuple-element.34) | copy-start | bytes 3145732
Sparse Core Ops, SparseCore 0:
  150.7 264.1 all-reduce.3
where the time goes:
time: 436 us; the launch traced here: 429 us
  waiting for transfers between devices  187 us (43%)
  blocking collectives  72 us (17%)
  matrix products  63.4 us (15%)
  local copies, waits for them, and re-layouts  56.7 us (13%)
  other arithmetic  22.6 us (5%)
  between operations  14.9 us (3%)
  starting transfers between devices  12.6 us (3%)
    psum x1, waiting for transfers between devices, body(): lax.psum((grad_gain, grad_query, grad_key, grad_value, grad_output), ('sp...  180 us
    psum x1, blocking collectives, body(): lax.psum((grad_gain, grad_query, grad_key, grad_value, grad_output), ('sp...  72 us
    dot_general x12, matrix products, matmul(): jnp.dot(left, right, precision=lax.Precision.HIGHEST, preferred_element_t...  30.5 us
    reshape x4, local copies, waits for them, and re-layouts, attention(): value_win.reshape(-1, PT, model_width)[block_index]  17.3 us
    dot_general x3, matrix products, attention(): jnp.einsum('phqk,pkhd->pqhd', probability, picked_values, precision=lax.P...  17 us
    reshape x4, local copies, waits for them, and re-layouts, attention(): key_win.reshape(-1, PT, model_width)[block_index]  16.9 us
    dot_general x3, matrix products, attention(): jnp.einsum('pqhd,pkhd->phqk', query_blocks, picked_keys, precision=lax.Pr...  15.9 us
    unnamed x58, local copies, waits for them, and re-layouts  8.76 us
  transfers between devices with their start and end apart: 5, of which 3 were waited for; matrix products, arithmetic and copies ran while one was open for 10% of the time, Pallas kernels for 0%

commit v1 on v0

--- a/solution.py
+++ b/solution.py
@@ -119,7 +119,7 @@
     d_norm, grad_gain = norm_pull(d_hidden)
     d_tokens = d_norm + cotangent
     grad_gain, grad_query, grad_key, grad_value, grad_output = lax.psum(
-        (grad_gain, grad_query, grad_key, grad_value, grad_output), ("space", "slab")
+        lax.psum((grad_gain, grad_query, grad_key, grad_value, grad_output), "space"), "slab"
     )
     return (result, d_tokens, grad_gain, grad_query, grad_key, grad_value, grad_output)
 

time: 436 us -> 510 us (1.17)
  blocking collectives: 72 us -> 137 us
  waiting for transfers between devices: 187 us -> 195 us
    psum x1 -> x2, blocking collectives: 72 us -> 137 us  [the longest x1 128 us: body(): lax.psum((grad_gain, grad_query, grad_key, grad_value, grad_output), 'spa...]
    psum x1 -> x2, waiting for transfers between devices: 180 us -> 189 us  [the longest x1 189 us: body(): lax.psum((grad_gain, grad_query, grad_key, grad_value, grad_output), 'spa...]
  transfers between devices with their start and end apart: 5 -> 6, of which waited for: 3 -> 3; matrix products, arithmetic and copies ran while one was open for 10% -> 8% of each run, Pallas kernels for 0% -> 0%
where the time goes in v1:
time: 510 us; the launch traced here: 502 us
  waiting for transfers between devices  195 us (38%)
  blocking collectives  137 us (27%)
  matrix products  63.1 us (12%)
  local copies, waits for them, and re-layouts  56.7 us (11%)
  other arithmetic  22.6 us (4%)
  between operations  15 us (3%)
  starting transfers between devices  12.9 us (3%)
    psum x1, waiting for transfers between devices, body(): lax.psum((grad_gain, grad_query, grad_key, grad_value, grad_output), 'spa...  189 us
    psum x1, blocking collectives, body(): lax.psum((grad_gain, grad_query, grad_key, grad_value, grad_output), 'spa...  128 us
    dot_general x12, matrix products, matmul(): jnp.dot(left, right, precision=lax.Precision.HIGHEST, preferred_element_t...  30.3 us
    reshape x4, local copies, waits for them, and re-layouts, attention(): value_win.reshape(-1, PT, model_width)[block_index]  17.3 us
    dot_general x3, matrix products, attention(): jnp.einsum('phqk,pkhd->pqhd', probability, picked_values, precision=lax.P...  17 us
    reshape x4, local copies, waits for them, and re-layouts, attention(): key_win.reshape(-1, PT, model_width)[block_index]  16.9 us
    dot_general x3, matrix products, attention(): jnp.einsum('pqhd,pkhd->phqk', query_blocks, picked_keys, precision=lax.Pr...  15.9 us
  transfers between devices with their start and end apart: 6, of which 3 were waited for; matrix products, arithmetic and copies ran while one was open for 8% of the time, Pallas kernels for 0%

profile of v1, /device:TPU:8, one launch (start us, length us, event | category | flops | bytes accessed | tf_op | source)
XLA Modules:
  0.0 502.5 jit_solution(12090228150470283688)
XLA Ops:
  9.8 2.2 fusion.56
  12.0 2.6 fusion.57
  15.6 7.5 %collective-permute-start.1 = (f32[256,1024]{1,0:T(8,128)}, f32[256,1024]{1,0:T(8,128)}, u32[]{:S(2)}, u32[]{:S(2)}) collective-permute-start(f32[256,1024]{1,0:T(8,128)} %pad_maximum_fusion.2), channel_id=1, source_target_pairs={{4,0},{8,4},{12,8},{16,12},{20,16},{24,20},{28,24},{32,28},{36,32}... | collective-permute-start | bytes 3145736 | tf_op jit(solution)/shard_map/ppermute | solution.py:19
  23.6 3.9 fusion.55
  29.7 3.0 fusion.62
  35.7 5.2 %collective-permute-done = f32[256,1024]{1,0:T(8,128)} collective-permute-done((f32[256,1024]{1,0:T(8,128)}, f32[256,1024]{1,0:T(8,128)}, u32[]{:S(2)}, u32[]{:S(2)}) %collective-permute-start) | collective-permute-done | bytes 1048608 | tf_op jit(solution)/shard_map/ppermute | solution.py:17
  44.3 3.4 gather_fusion
  47.8 4.9 reshape.226
  52.6 3.8 copy.41
  58.4 4.4 reshape.227
  62.8 3.9 copy.40
  66.7 5.7 %fusion.1 = (f32[2,8,128]{2,1,0:T(8,128)S(1)}, f32[2,8,128,512]{3,2,1,0:T(8,128)S(1)}) fusion(pred[2,512]{1,0:T(4,128)(4,1)S(1)} %bitcast.73, f32[2,512,8,64]{1,3,2,0:T(8,128)} %copy.40, f32[2,128,8,64]{1,0,3,2:T(2,128)S(1)} %copy-done.9), kind=kOutput, calls=%fused_computation.15 | convolution fusion | flops 808450048 | bytes 6824960 | tf_op jit(solution)/shard_map/jvp(pqhd,pkhd->phqk)/dot_general | solution.py:54
  73.8 4.5 fusion.14
  78.3 5.6 %convert_reduce_fusion = (f32[2,8,128]{2,1,0:T(8,128)S(1)}, pred[2,8,128,512]{3,2,1,0:T(32,128)(4,1)S(1)}, f32[2,8,128]{2,1,0:T(8,128)S(1)}, f32[2,8,128,512]{3,2,1,0:T(8,128)S(1)}) fusion(f32[2,8,128]{2,1,0:T(8,128)S(1)} %get-tuple-element.28, f32[2,8,128,512]{3,2,1,0:T(8,128)S(1)} %get-tuple-element.29, pred[2,512]{1,0:T(4,128)(4,1)S(1)} %bitcast.76, ...), kind=kOutput, calls=%fused_computation.5 | convolution fusion | flops 814739456 | bytes 12092416 | tf_op jit(solution)/shard_map/transpose(jvp(phqk,pkhd->pqhd))/dot_general | solution.py:62
  88.0 4.6 fusion.15
  92.7 3.8 copy.56
  96.5 4.8 reshape.224
  101.3 3.8 copy.57
  105.1 4.8 reshape.225
  111.4 5.0 %scatter_fusion = f32[6,128,512]{2,1,0:T(8,128)} fusion(f32[6,128,512]{2,1,0:T(8,128)} %broadcast.104.clone, s32[8]{0:T(128)S(1)} %reshape.186, f32[8,128,512]{2,1,0:T(8,128)} %reshape.224), kind=kCustom, calls=%fused_computation.2 | custom fusion | flops 524288 | bytes 6291488 | tf_op jit(solution)/shard_map/transpose(jvp())/scatter-add | solution.py:47
  116.6 3.4 scatter_fusion.1
  121.6 5.0 %collective-permute-start.2 = (f32[256,1024]{1,0:T(8,128)S(1)}, f32[256,1024]{1,0:T(8,128)S(1)}, u32[]{:S(2)}, u32[]{:S(2)}) collective-permute-start(f32[256,1024]{1,0:T(8,128)S(1)} %get-tuple-element.24), channel_id=1, source_target_pairs={{0,252},{4,0},{8,4},{12,8},{16,12},{20,16},{24,20},{28,24},{32,28}... | collective-permute-start | bytes 3145736 | tf_op jit(solution)/shard_map/ppermute | solution.py:29
  126.6 6.9 %fusion.16 = f32[2,128,8,64]{1,3,2,0:T(8,128)S(1)} fusion(f32[2,512,8,64]{1,3,2,0:T(8,128)} %copy.41, f32[2,8,128]{2,1,0:T(8,128)S(1)} %fusion.45, f32[2,8,128,512]{3,2,1,0:T(8,128)S(1)} %copy-done.5, f32[2,8,128]{2,1,0:T(8,128)S(1)} %get-tuple-element.28, pred[2,512]{1,0:T(4,128)(4,1)S(1)} %bitcast.79), kind=kOutput, calls=%fused_computation.32 | convolution fusion | flops 809500672 | bytes 6833152 | tf_op jit(solution)/shard_map/jvp(phqk,pkhd->pqhd)/dot_general | solution.py:62
  134.1 5.6 %fusion.17 = f32[2,128,8,64]{1,3,2,0:T(8,128)S(1)} fusion(f32[2,512,8,64]{1,3,2,0:T(8,128)S(1)} %copy-done.6, f32[2,8,128,512]{3,2,1,0:T(8,128)S(1)} %copy-done.3, pred[2,8,128,512]{3,2,1,0:T(32,128)(4,1)S(1)} %copy-done.17, f32[2,8,128]{2,1,0:T(8,128)S(1)} %negate_divide_fusion, pred[2,512]{1,0:T(4,128)(4,1)S(1)} %bitcast.80), kind=kOutput, calls=%fused_computation.36 | convolution fusion | flops 809500672 | bytes 7873536 | tf_op jit(solution)/shard_map/transpose(jvp(pqhd,pkhd->phqk))/dot_general | solution.py:54
  142.1 2.9 fusion.22
  150.9 189.2 %all-reduce.6.cloned.1.call-done = (f32[512,512]{1,0:T(8,128)}, f32[512,512]{1,0:T(8,128)}, f32[512,512]{1,0:T(8,128)}, f32[512,512]{1,0:T(8,128)}) async-done(((f32[512,512]{1,0:T(8,128)}, f32[512,512]{1,0:T(8,128)}, f32[512,512]{1,0:T(8,128)}, f32[512,512]{1,0:T(8,128)}), (f32[512,512]{1,0:T(8,128)}, f32[512,512]{1,0:T(8,128)}, f32[512,512]{1,0:T(8,128)}, ...) | async-done | bytes 4194320 | tf_op jit(solution)/shard_map/psum | solution.py:122
  340.2 3.4 fusion.24
  343.6 3.1 convolution_add_fusion.2
  349.6 127.5 %psum.70 = f32[512]{0:T(512)S(1)} all-reduce(f32[512]{0:T(512)S(1)} %get-tuple-element.7), channel_id=1, replica_groups=mesh['space'=64,'slab'=4] {'space'}, use_global_device_ids=true, to_apply=%region_12.13 | all-reduce | flops 512 | bytes 4096 | tf_op jit(solution)/shard_map/psum | solution.py:122
  477.1 9.2 %psum.71 = f32[512]{0:T(512)} all-reduce(f32[512]{0:T(512)S(1)} %psum.70), channel_id=1, replica_groups=mesh['space'=64,'slab'=4] {'slab'}, use_global_device_ids=true, to_apply=%region_13.14 | all-reduce | flops 512 | bytes 4096 | tf_op jit(solution)/shard_map/psum | solution.py:121
  488.6 2.4 copy.111
  491.0 2.3 copy.112
  (103 shorter events, 39.2 us)
Async XLA Ops:
  7.2 2.6 copy-start
  7.2 16.4 %copy-start.1 = (f32[256,512]{1,0:T(8,128)S(1)}, f32[256,512]{1,0:T(8,128)}, u32[]{:S(2)}) copy-start(f32[256,512]{1,0:T(8,128)} %param.9) | copy-start | bytes 1572868
  7.2 16.4 %copy-start.23 = (f32[512]{0:T(512)S(1)}, f32[512]{0:T(512)}, u32[]{:S(2)}) copy-start(f32[512]{0:T(512)} %param.10) | copy-start | bytes 6148
  7.2 16.0 %copy-start.24 = (s32[2,3]{1,0:T(2,128)S(1)}, s32[2,3]{1,0:T(2,128)}, u32[]{:S(2)}) copy-start(s32[2,3]{1,0:T(2,128)} %param.15) | copy-start | bytes 76
  7.2 16.2 %copy-start.25 = (s32[2]{0:T(128)S(1)}, s32[2]{0:T(128)}, u32[]{:S(2)}) copy-start(s32[2]{0:T(128)} %param.16) | copy-start | bytes 28
  7.2 332.9 %all-reduce.6.cloned.1.call-start = ((), (), s32[]{:S(2)}) async-start(), calls=%async_computation | async-start | bytes 8388608 | tf_op jit(solution)/shard_map/psum | solution.py:122
  12.0 17.7 %copy-start.13 = (f32[256,512]{1,0:T(8,128)S(1)}, f32[256,512]{1,0:T(8,128)}, u32[]{:S(2)}) copy-start(f32[256,512]{1,0:T(8,128)} %param.17) | copy-start | bytes 1572868
  15.6 20.1 %collective-permute-start.1 = (f32[256,1024]{1,0:T(8,128)}, f32[256,1024]{1,0:T(8,128)}, u32[]{:S(2)}, u32[]{:S(2)}) collective-permute-start(f32[256,1024]{1,0:T(8,128)} %pad_maximum_fusion.2), channel_id=1, source_target_pairs={{4,0},{8,4},{12,8},{16,12},{20,16},{24,20},{28,24},{32,28},{36,32}... | collective-permute-start | bytes 3145736 | tf_op jit(solution)/shard_map/ppermute | solution.py:19
  23.1 17.9 %collective-permute-start = (f32[256,1024]{1,0:T(8,128)}, f32[256,1024]{1,0:T(8,128)}, u32[]{:S(2)}, u32[]{:S(2)}) collective-permute-start(f32[256,1024]{1,0:T(8,128)} %pad_maximum_fusion.2), channel_id=1, source_target_pairs={{0,4},{4,8},{8,12},{12,16},{16,20},{20,24},{24,28},{28,32},{32,36}... | collective-permute-start | bytes 3145736 | tf_op jit(solution)/shard_map/ppermute | solution.py:17
  62.8 3.9 copy-start.9
  66.7 7.1 %copy-start.22 = (f32[2,128,8,64]{1,0,3,2:T(2,128)S(1)}, f32[2,128,8,64]{1,0,3,2:T(2,128)}, u32[]{:S(2)}) copy-start(f32[2,128,8,64]{1,0,3,2:T(2,128)} %reshape.178) | copy-start | bytes 1572868
  72.4 11.5 %copy-start.4 = (f32[2,8,128,512]{3,2,1,0:T(8,128)}, f32[2,8,128,512]{3,2,1,0:T(8,128)S(1)}, u32[]{:S(2)}) copy-start(f32[2,8,128,512]{3,2,1,0:T(8,128)S(1)} %get-tuple-element.29) | copy-start | bytes 12582916
  73.8 4.5 copy-start.19
  83.8 2.2 copy-start.16
  86.0 2.0 copy-start.2
  119.9 6.7 %copy-start.5 = (f32[2,8,128,512]{3,2,1,0:T(8,128)S(1)}, f32[2,8,128,512]{3,2,1,0:T(8,128)}, u32[]{:S(2)}) copy-start(f32[2,8,128,512]{3,2,1,0:T(8,128)} %copy-done.4) | copy-start | bytes 12582916
  121.5 23.5 %collective-permute-start.3 = (f32[256,1024]{1,0:T(8,128)S(1)}, f32[256,1024]{1,0:T(8,128)S(1)}, u32[]{:S(2)}, u32[]{:S(2)}) collective-permute-start(f32[256,1024]{1,0:T(8,128)S(1)} %get-tuple-element.25), channel_id=1, source_target_pairs={{0,4},{4,8},{8,12},{12,16},{16,20},{20,24},{24,28},{28,32},{32,36}... | collective-permute-start | bytes 3145736 | tf_op jit(solution)/shard_map/ppermute | solution.py:29
  121.6 12.4 %copy-start.3 = (f32[2,8,128,512]{3,2,1,0:T(8,128)S(1)}, f32[2,8,128,512]{3,2,1,0:T(8,128)}, u32[]{:S(2)}) copy-start(f32[2,8,128,512]{3,2,1,0:T(8,128)} %copy-done.2) | copy-start | bytes 12582916
  121.6 12.4 %copy-start.6 = (f32[2,512,8,64]{1,3,2,0:T(8,128)S(1)}, f32[2,512,8,64]{1,3,2,0:T(8,128)}, u32[]{:S(2)}) copy-start(f32[2,512,8,64]{1,3,2,0:T(8,128)} %copy.40) | copy-start | bytes 6291460
  121.6 12.4 %copy-start.17 = (pred[2,8,128,512]{3,2,1,0:T(32,128)(4,1)S(1)}, pred[2,8,128,512]{3,2,1,0:T(32,128)(4,1)}, u32[]{:S(2)}) copy-start(pred[2,8,128,512]{3,2,1,0:T(32,128)(4,1)} %copy-done.16) | copy-start | bytes 3145732
  121.6 23.4 %collective-permute-start.2 = (f32[256,1024]{1,0:T(8,128)S(1)}, f32[256,1024]{1,0:T(8,128)S(1)}, u32[]{:S(2)}, u32[]{:S(2)}) collective-permute-start(f32[256,1024]{1,0:T(8,128)S(1)} %get-tuple-element.24), channel_id=1, source_target_pairs={{0,252},{4,0},{8,4},{12,8},{16,12},{20,16},{24,20},{28,24},{32,28}... | collective-permute-start | bytes 3145736 | tf_op jit(solution)/shard_map/ppermute | solution.py:29
  134.0 6.0 %copy-start.10 = (f32[2,128,8,64]{1,0,3,2:T(2,128)}, f32[2,128,8,64]{1,0,3,2:T(2,128)S(1)}, u32[]{:S(2)}) copy-start(f32[2,128,8,64]{1,0,3,2:T(2,128)S(1)} %copy.42) | copy-start | bytes 1572868
  134.0 6.0 %copy-start.14 = (f32[256,512]{1,0:T(8,128)S(1)}, f32[256,512]{1,0:T(8,128)}, u32[]{:S(2)}) copy-start(f32[256,512]{1,0:T(8,128)} %param.17) | copy-start | bytes 1572868
  140.1 4.9 copy-start.12
  146.3 2.1 copy-start.7
  150.6 193.0 %copy-start.11 = (f32[2,128,8,64]{1,0,3,2:T(2,128)S(1)}, f32[2,128,8,64]{1,0,3,2:T(2,128)}, u32[]{:S(2)}) copy-start(f32[2,128,8,64]{1,0,3,2:T(2,128)} %copy-done.10) | copy-start | bytes 1572868
  150.6 338.0 %all-reduce.8.cloned.1.call-start = ((), (), s32[]{:S(2)}) async-start(), calls=%async_computation.1 | async-start | bytes 8388608 | tf_op jit(solution)/shard_map/psum | solution.py:121
  340.1 6.5 %copy-start.8 = (f32[256,1024]{1,0:T(8,128)S(1)}, f32[256,1024]{1,0:T(8,128)}, u32[]{:S(2)}) copy-start(f32[256,1024]{1,0:T(8,128)} %copy-done.7) | copy-start | bytes 3145732
  340.2 6.5 %copy-start.18 = (f32[512,512]{1,0:T(8,128)S(1)}, f32[512,512]{1,0:T(8,128)}, u32[]{:S(2)}) copy-start(f32[512,512]{1,0:T(8,128)} %param.12) | copy-start | bytes 3145732
  346.7 141.0 %copy-start.15 = (f32[256,512]{1,0:T(8,128)S(1)}, f32[256,512]{1,0:T(8,128)}, u32[]{:S(2)}) copy-start(f32[256,512]{1,0:T(8,128)} %param.17) | copy-start | bytes 1572868
  488.6 4.7 copy-start.21
  488.6 5.7 %copy-start.20 = (f32[512,512]{1,0:T(8,128)S(1)}, f32[512,512]{1,0:T(8,128)}, u32[]{:S(2)}) copy-start(f32[512,512]{1,0:T(8,128)} %get-tuple-element.38) | copy-start | bytes 3145732
Sparse Core Ops, SparseCore 0:
  150.7 189.3 all-reduce.5
  342.8 96.1 all-reduce.7
